TPU v7x, 32 devices: a whole 2x2x4 slice. The times are simulated.
32 devices in a mesh: group: 2 (over x), ctx: 8 (over z, y), exp: 2 (over core).
Axes of the slice: x: 2, y: 2, z: 4, core: 2. Of those that a mesh axis runs over, the one named last changes fastest.
Arguments:
- prompt_query: bfloat16 [2, 2, 2048, 2048], P('group', 'exp', 'ctx'), may hold values from -6 to 6
- prompt_keys: bfloat16 [2, 2, 2048, 256], P('group', 'exp', 'ctx'), may hold values from -6 to 6
- prompt_values: bfloat16 [2, 2, 2048, 256], P('group', 'exp', 'ctx'), may hold values from -24 to 24
- lengths: int32 [2, 2], P(None, 'exp'), may hold values from 1025 to 2048
- decode_query: bfloat16 [2, 2, 128, 2048], P('group', 'exp', None, 'ctx'), may hold values from -6 to 6
- fresh_keys: bfloat16 [2, 2, 128, 256], P('group', 'exp'), may hold values from -6 to 6
- fresh_values: bfloat16 [2, 2, 128, 256], P('group', 'exp'), may hold values from -24 to 24
- x_dec: bfloat16 [2, 2, 128, 2048], P('group', 'exp', 'ctx'), may hold values from -0.59765625 to 0.59765625
- w_out: bfloat16 [2048, 2048], P('ctx'), may hold values from -0.125 to 0.125
- norm_gain: bfloat16 [2048], replicated, may hold values from 0.5 to 1.5
- w_gate_up: bfloat16 [16, 2048, 1536], P(('ctx', 'exp')), may hold values from -0.125 to 0.125
- w_down: bfloat16 [16, 768, 2048], P(('ctx', 'exp')), may hold values from -0.21875 to 0.21875
- expert_ids: int32 [2, 2, 128, 8], P('group', 'exp', 'ctx'), may hold values from 0 to 15, all different within a row; in each aligned block of 16 rows (0 to 15, 16 to 31, ..., all dimensions but the last counted through in order) at most 16 rows name the same one
- gate_weights: float32 [2, 2, 128, 8], P('group', 'exp', 'ctx'), may hold values from 0.1 to 1
Outputs:
- prompt_attention: bfloat16 [2, 2, 2048, 2048], P('group', 'exp', 'ctx')
- out_dec: bfloat16 [2, 2, 128, 2048], P('group', 'exp', 'ctx')
Inputs may be any that keep to these rules, and one draw needn't show every extreme that they name: `expert_ids`: the 8 experts of a row differ; among the rows of one device no expert is named more than 16 times.
All inputs are finite; a program needn't handle non-finite values.
Results may differ from a plain program's by a relative error of at most 0.025.
Values may be sent and summed in bfloat16 or wider, within the bound.
A program may use at most 128 MiB of HBM per device.

v0:
```python
import math
import jax
import jax.numpy as jnp
from jax import lax
from jax.sharding import PartitionSpec as P

HEAD_SIZE = 128
QUERY_HEADS = 16
KEY_VALUE_HEADS = 2
NEGATIVE_LIMIT = -1e30
EPSILON = 1e-06


def from_partner(block, axis, apart):
    count = lax.axis_size(axis)
    route = []
    for low in range(count):
        high = low | 1 << apart
        if high != low and high < count:
            route += [(low, high), (high, low)]
    return lax.ppermute(block, axis, route)


def blockwise(update, carried, key_row_list, value_row_list, positions, usable):
    row_count = key_row_list.shape[0]
    stride = math.gcd(row_count, 512)
    splits = row_count // stride

    def advance(status, members):
        return (update(status, *members), None)

    shaped = (
        key_row_list.reshape(splits, stride, key_row_list.shape[1]),
        value_row_list.reshape(splits, stride, value_row_list.shape[1]),
        positions.reshape(splits, stride),
        usable.reshape(splits, stride),
    )
    carried, unused_out = lax.scan(advance, carried, shaped)
    return carried


def body(
    prompt_query,
    prompt_keys,
    prompt_values,
    lengths,
    decode_query,
    fresh_keys,
    fresh_values,
    x_dec,
    w_out,
    norm_gain,
    w_gate_up,
    w_down,
    expert_ids,
    gate_weights,
):
    group_width = QUERY_HEADS // KEY_VALUE_HEADS
    scaling = HEAD_SIZE ** (-0.5)
    my_group = lax.axis_index("group")
    ctx_index = lax.axis_index("ctx")
    ctx_count = lax.axis_size("ctx")
    length_list = lengths[:, 0]
    length_mine = lax.dynamic_index_in_dim(length_list, my_group, keepdims=False)
    length_other = lax.dynamic_index_in_dim(length_list, 1 - my_group, keepdims=False)
    token_rows = prompt_query.shape[2]
    prompt_len = token_rows * ctx_count
    query_tensor = prompt_query[0, 0].reshape(token_rows, KEY_VALUE_HEADS, group_width, HEAD_SIZE)
    query_pos = ctx_index * token_rows + lax.iota(jnp.int32, token_rows)
    query_limit = jnp.minimum(length_mine, ctx_index * token_rows + token_rows)
    local_heads = decode_query.shape[3] // HEAD_SIZE
    samples = decode_query.shape[2]
    dec_queries = decode_query[0, 0].reshape(samples, local_heads, HEAD_SIZE)
    kv_head = ctx_index * local_heads // group_width

    def prefill_step(status, key_row_list, value_row_list, positions, usable):
        usable = usable & (positions < query_limit)

        def prefill_compute(carried):
            run_max, run_sum, weighted = carried
            key_parts = key_row_list.reshape(-1, KEY_VALUE_HEADS, HEAD_SIZE)
            value_parts = value_row_list.reshape(-1, KEY_VALUE_HEADS, HEAD_SIZE)
            scores = (
                jnp.einsum(
                    "qhgd,khd->hgqk", query_tensor, key_parts, preferred_element_type=jnp.float32
                )
                * scaling
            )
            keep_mask = usable[None, :] & (positions[None, :] <= query_pos[:, None])
            scores = jnp.where(keep_mask[None, None], scores, NEGATIVE_LIMIT)
            new_max = jnp.maximum(run_max, scores.max(-1))
            rescale = jnp.exp(run_max - new_max)
            weights = jnp.where(keep_mask[None, None], jnp.exp(scores - new_max[..., None]), 0.0)
            run_sum = rescale * run_sum + weights.sum(-1)
            weighted = rescale[..., None] * weighted + jnp.einsum(
                "hgqk,khd->hgqd",
                weights.astype(jnp.bfloat16),
                value_parts,
                preferred_element_type=jnp.float32,
            )
            return (new_max, run_sum, weighted)

        return lax.cond(jnp.any(usable), prefill_compute, lambda carried: carried, status)

    def make_decode():

        def decode_step(status, key_row_list, value_row_list, positions, usable):
            usable = usable & (positions < length_other)

            def decode_compute(carried):
                run_max, run_sum, weighted = carried
                scores = (
                    jnp.einsum(
                        "shd,kd->hsk", dec_queries, key_row_list, preferred_element_type=jnp.float32
                    )
                    * scaling
                )
                scores = jnp.where(usable[None, None], scores, NEGATIVE_LIMIT)
                new_max = jnp.maximum(run_max, scores.max(-1))
                rescale = jnp.exp(run_max - new_max)
                weights = jnp.where(usable[None, None], jnp.exp(scores - new_max[..., None]), 0.0)
                run_sum = rescale * run_sum + weights.sum(-1)
                weighted = rescale[..., None] * weighted + jnp.einsum(
                    "hsk,kd->hsd",
                    weights.astype(jnp.bfloat16),
                    value_row_list,
                    preferred_element_type=jnp.float32,
                )
                return (new_max, run_sum, weighted)

            return lax.cond(jnp.any(usable), decode_compute, lambda carried: carried, status)

        return decode_step

    decode_step = make_decode()
    pre_init = (
        jnp.full((KEY_VALUE_HEADS, group_width, token_rows), NEGATIVE_LIMIT, jnp.float32),
        jnp.zeros((KEY_VALUE_HEADS, group_width, token_rows), jnp.float32),
        jnp.zeros((KEY_VALUE_HEADS, group_width, token_rows, HEAD_SIZE), jnp.float32),
    )
    dec_init = (
        jnp.full((local_heads, samples), NEGATIVE_LIMIT, jnp.float32),
        jnp.zeros((local_heads, samples), jnp.float32),
        jnp.zeros((local_heads, samples, HEAD_SIZE), jnp.float32),
    )
    far_keys, far_values = from_partner((prompt_keys, prompt_values), "group", 0)
    peer_heads = lax.iota(jnp.int32, ctx_count) * local_heads // group_width
    key_chosen = jnp.take(
        far_keys[0, 0].reshape(token_rows, KEY_VALUE_HEADS, HEAD_SIZE), peer_heads, axis=1
    )
    value_chosen = jnp.take(
        far_values[0, 0].reshape(token_rows, KEY_VALUE_HEADS, HEAD_SIZE), peer_heads, axis=1
    )
    head_keys, head_values = (
        lax.all_to_all(key_chosen, "ctx", split_axis=1, concat_axis=0, tiled=True),
        lax.all_to_all(value_chosen, "ctx", split_axis=1, concat_axis=0, tiled=True),
    )
    key_piece = lax.all_gather(prompt_keys, "ctx", axis=2, tiled=True)
    value_piece = lax.all_gather(prompt_values, "ctx", axis=2, tiled=True)
    row_count = key_piece.shape[2]
    positions = lax.iota(jnp.int32, row_count)
    pre_state = blockwise(
        prefill_step, pre_init, key_piece[0, 0], value_piece[0, 0], positions, positions >= 0
    )
    all_positions = lax.iota(jnp.int32, prompt_len)
    dec_state = blockwise(
        make_decode(),
        dec_init,
        head_keys.reshape(prompt_len, HEAD_SIZE),
        head_values.reshape(prompt_len, HEAD_SIZE),
        all_positions,
        all_positions >= 0,
    )
    pre_max, pre_sum, pre_weighted = pre_state
    prompt_attn = pre_weighted / jnp.where(pre_sum > 0, pre_sum, 1.0)[..., None]
    prompt_attn = jnp.transpose(prompt_attn, (2, 0, 1, 3)).reshape(
        token_rows, QUERY_HEADS * HEAD_SIZE
    )
    prompt_attn = jnp.where((query_pos < length_mine)[:, None], prompt_attn, 0.0).astype(
        jnp.bfloat16
    )
    prompt_attention = prompt_attn.reshape(1, 1, token_rows, QUERY_HEADS * HEAD_SIZE)
    dec_max, dec_sum, dec_weighted = dec_state
    own_keys = lax.dynamic_slice_in_dim(fresh_keys[0, 0], kv_head * HEAD_SIZE, HEAD_SIZE, 1)
    own_values = lax.dynamic_slice_in_dim(fresh_values[0, 0], kv_head * HEAD_SIZE, HEAD_SIZE, 1)
    own_score = (
        jnp.einsum("shd,sd->hs", dec_queries, own_keys, preferred_element_type=jnp.float32)
        * scaling
    )
    final_max = jnp.maximum(dec_max, own_score)
    rescale = jnp.exp(dec_max - final_max)
    own_weight = jnp.exp(own_score - final_max)
    dec_sum = rescale * dec_sum + own_weight
    dec_weighted = (
        rescale[..., None] * dec_weighted
        + own_weight.astype(jnp.bfloat16).astype(jnp.float32)[..., None]
        * own_values.astype(jnp.float32)[None]
    )
    dec_attn = (dec_weighted / dec_sum[..., None]).astype(jnp.bfloat16)
    dec_attn = jnp.transpose(dec_attn, (1, 0, 2)).reshape(samples, local_heads * HEAD_SIZE)
    row_count = x_dec.shape[2]
    projected = lax.psum_scatter(
        jnp.dot(dec_attn, w_out, preferred_element_type=jnp.float32).astype(jnp.bfloat16),
        "ctx",
        scatter_dimension=0,
        tiled=True,
    ).astype(jnp.float32)
    residual = x_dec[0, 0].astype(jnp.float32) + projected
    normed = (
        residual
        * lax.rsqrt(jnp.mean(residual * residual, -1, keepdims=True) + EPSILON)
        * norm_gain.astype(jnp.float32)
    ).astype(jnp.bfloat16)
    model_width = normed.shape[1]
    top_count = expert_ids.shape[3]
    n_ctx = lax.axis_size("ctx")
    n_exp = lax.axis_size("exp")
    experts_all = w_gate_up.shape[0] * n_ctx * n_exp
    capacity = max(2, 2 * row_count * top_count // experts_all)
    flat_ids = expert_ids[0, 0].reshape(-1)
    one_hot = (flat_ids[:, None] == lax.iota(jnp.int32, experts_all)[None, :]).astype(jnp.int32)
    earlier = jnp.cumsum(one_hot, 0) - one_hot
    slot_rank = jnp.sum(earlier * one_hot, 1)
    target = flat_ids * capacity + slot_rank
    placing = (
        lax.iota(jnp.int32, experts_all * capacity)[:, None, None]
        == target.reshape(row_count, top_count)[None]
    ).any(-1)
    buffer = jnp.dot(
        placing.astype(jnp.bfloat16), normed, preferred_element_type=jnp.float32
    ).astype(jnp.bfloat16)
    buffer = buffer.reshape(experts_all, capacity, model_width)
    arrived = lax.all_to_all(buffer, ("ctx", "exp"), split_axis=0, concat_axis=0, tiled=True)
    flat_rows = arrived.reshape(-1, model_width)
    mixed = jnp.dot(flat_rows, w_gate_up[0], preferred_element_type=jnp.float32)
    hidden_units = mixed.shape[1] // 2
    hidden = (jax.nn.silu(mixed[:, :hidden_units]) * mixed[:, hidden_units:]).astype(jnp.bfloat16)
    produced = jnp.dot(hidden, w_down[0], preferred_element_type=jnp.float32).astype(jnp.bfloat16)
    outputs = produced.reshape(arrived.shape)
    returned = lax.all_to_all(outputs, ("ctx", "exp"), split_axis=0, concat_axis=0, tiled=True)
    picked = returned.reshape(experts_all * capacity, model_width)[target]
    gate_values = gate_weights[0, 0]
    moe = jnp.sum(
        picked.reshape(row_count, top_count, model_width).astype(jnp.float32)
        * gate_values[..., None],
        1,
    )
    out_dec = (residual + moe).astype(jnp.bfloat16).reshape(1, 1, row_count, model_width)
    return (prompt_attention, out_dec)


def solution(mesh):
    in_specs = (
        P("group", "exp", "ctx", None),
        P("group", "exp", "ctx", None),
        P("group", "exp", "ctx", None),
        P(None, "exp"),
        P("group", "exp", None, "ctx"),
        P("group", "exp", None, None),
        P("group", "exp", None, None),
        P("group", "exp", "ctx", None),
        P("ctx", None),
        P(),
        P(("ctx", "exp"), None, None),
        P(("ctx", "exp"), None, None),
        P("group", "exp", "ctx", None),
        P("group", "exp", "ctx", None),
    )
    out_specs = (P("group", "exp", "ctx", None), P("group", "exp", "ctx", None))
    return jax.shard_map(body, mesh=mesh, in_specs=in_specs, out_specs=out_specs, check_vma=False)
```

profile of v0, /device:TPU:25, one launch (start us, length us, event | category | flops | bytes accessed | tf_op | source)
XLA Modules:
  0.0 324.3 jit_solution(11437767902272269892)
XLA Ops:
  22.6 16.7 %all_to_all.40 = bf16[256,8,128]{2,0,1:T(8,128)(2,1)} all-to-all(bf16[256,8,128]{2,0,1:T(8,128)(2,1)S(1)} %get-tuple-element.486), channel_id=1, replica_groups=mesh['group'=2,'ctx'=8,'exp'=2] {'ctx'}, dimensions={1} | all-to-all | bytes 1048576 | tf_op jit(solution)/shard_map/all_to_all | solution.py:155
  39.3 6.3 %all-to-all-start.1 = ((bf16[256,8,128]{2,0,1:T(8,128)(2,1)}), bf16[256,8,128]{2,0,1:T(8,128)(2,1)}, u32[]{:S(2)}, u32[]{:S(2)}) async-start(bf16[256,8,128]{2,0,1:T(8,128)(2,1)} %get-tuple-element.485), calls=%async_computation.1 | async-start | bytes 1048576 | tf_op jit(solution)/shard_map/all_to_all | solution.py:156
  48.9 8.3 %all-to-all-done.1 = bf16[256,8,128]{2,0,1:T(8,128)(2,1)} async-done(((bf16[256,8,128]{2,0,1:T(8,128)(2,1)}), bf16[256,8,128]{2,0,1:T(8,128)(2,1)}, u32[]{:S(2)}, u32[]{:S(2)}) %all-to-all-start.1) | async-done | bytes 524320 | tf_op jit(solution)/shard_map/all_to_all | solution.py:156
  57.3 16.7 %while.31 = (s32[]{:T(128)}, f32[2,128]{1,0:T(2,128)S(1)}, f32[2,128]{1,0:T(2,128)S(1)}, f32[2,128,128]{2,1,0:T(8,128)S(1)}, s32[4,512]{1,0:T(4,128)S(1)}, /*ind...) while((s32[]{:T(128)}, f32[2,128]{1,0:T(2,128)S(1)}, ...), condition=%wide.region_13.15_spmd, body=%wide.region_7.14_spmd.sunk | while | flops 68355584 | bytes 2185460 | solution.py:38
  59.4 2.7 conditional.5
  64.2 2.7 conditional.5
  69.1 2.7 conditional.5
  81.0 61.8 %reduce-scatter.2.cloned.1.call-done = bf16[16,2048]{1,0:T(8,128)(2,1)} async-done(((bf16[128,2048]{1,0:T(8,128)(2,1)}), bf16[16,2048]{1,0:T(8,128)(2,1)}) %reduce-scatter.2.cloned.1.call-update) | async-done | bytes 65552 | tf_op jit(solution)/shard_map/reduce_scatter | solution.py:202
  146.1 7.9 %all-to-all-start.2 = ((bf16[16,16,2048]{2,1,0:T(8,128)(2,1)}), bf16[16,16,2048]{2,1,0:T(8,128)(2,1)}, u32[]{:S(2)}, u32[]{:S(2)}) async-start(bf16[16,16,2048]{2,1,0:T(8,128)(2,1)} %bitcast.131), calls=%async_computation.3 | async-start | bytes 2097152 | tf_op jit(solution)/shard_map/all_to_all | solution.py:233
  160.8 33.7 %all-gather.3.cloned.1.call-done = bf16[1,1,2048,256]{3,2,1,0:T(8,128)(2,1)} async-done(((bf16[1,1,256,256]{3,2,1,0:T(8,128)(2,1)}), bf16[1,1,2048,256]{3,2,1,0:T(8,128)(2,1)}) %all-gather.3.cloned.1.call-update) | async-done | bytes 1048592 | tf_op jit(solution)/shard_map/all_gather | solution.py:158
  196.7 38.9 %all-gather.5.cloned.1.call-done = bf16[1,1,2048,256]{3,2,1,0:T(8,128)(2,1)} async-done(((bf16[1,1,256,256]{3,2,1,0:T(8,128)(2,1)}), bf16[1,1,2048,256]{3,2,1,0:T(8,128)(2,1)}) %all-gather.5.cloned.1.call-update) | async-done | bytes 1048592 | tf_op jit(solution)/shard_map/all_gather | solution.py:159
  237.8 4.9 %fusion.28 = f32[256,1536]{1,0:T(8,128)S(1)} fusion(bf16[256,2048]{1,0:T(8,128)(2,1)} %bitcast.38, bf16[1,2048,1536]{2,1,0:T(8,128)(2,1)} %param.34), kind=kOutput, calls=%fused_computation.43 | convolution fusion | flops 1610612736 | bytes 8912896 | tf_op jit(solution)/shard_map/dot_general | solution.py:235
  244.8 8.3 %all-to-all-start.3 = ((bf16[16,16,2048]{2,1,0:T(8,128)(2,1)}), bf16[16,16,2048]{2,1,0:T(8,128)(2,1)}, u32[]{:S(2)}, u32[]{:S(2)}) async-start(bf16[16,16,2048]{2,1,0:T(8,128)(2,1)} %bitcast.134), calls=%async_computation.4 | async-start | bytes 2097152 | tf_op jit(solution)/shard_map/all_to_all | solution.py:240
  254.6 49.1 %while.32 = (s32[]{:T(128)}, f32[2,8,256]{2,1,0:T(8,128)S(1)}, f32[2,8,256]{2,1,0:T(8,128)S(1)}, f32[2,8,256,128]{3,2,1,0:T(8,128)}, s32[4,512]{1,0:T(4,128)S(1)...) while((s32[]{:T(128)}, f32[2,8,256]{2,1,0:T(8,128)S(1)}, ...), condition=%wide.region_6.7_spmd.clone, body=%wide.region_0.0_spmd.clone.sunk | while | flops 1102324992 | bytes 49558864 | solution.py:38
  256.0 11.0 %conditional.6 = ((f32[2,8,256]{2,1,0:T(8,128)S(1)}, f32[2,8,256]{2,1,0:T(8,128)S(1)}, f32[2,8,256,128]{3,2,1,0:T(8,128)})) conditional(s32[]{:T(128)} %convert_element_type.148, (f32[2,8,256]{2,1,0:T(8,128)S(1)}, f32[2,8,256]{2,1,0:T(8,128)S(1)}, f32[2,8,256,128]{3,2,1,0:T(8,128)}) %tuple.99, (pred[512]{0:T(512)(128)(4,1)S(1)}, s32[512]{0:T(512)S(1)}, ...), branch_computations={%region_2.2_spmd, %region_3.5_spmd} | conditional | flops 1102323968 | bytes 49550944 | solution.py:103
  257.3 2.7 fusion.2
  262.1 3.5 %multiply_add_fusion = f32[2,8,256,128]{3,2,1,0:T(8,128)S(1)} fusion(f32[2,8,256,128]{3,2,1,0:T(8,128)S(1)} %copy-done.1, bf16[512,2,128,1]{0,2,3,1:T(8,128)(2,1)S(1)} %bitcast.130, f32[2,512,256,8]{2,1,3,0:T(8,128)S(1)} %get-tuple-element.479, f32[2,8,256]{2,1,0:T(8,128)S(1)} %max.10, pred[256,512]{0,1:T(8,128)(4,1)S(1)} %compare_and_fusion, ...), kind=kOutput, calls=%fused_computation.11 | convolution fusion | flops 548405248 | bytes 13008896 | tf_op jit(solution)/shard_map/while/body/eval_jaxpr/cond/branch_1_fun/hgqk,khd->hgqd/dot_general | solution.py:95
  268.2 11.0 %conditional.6 = ((f32[2,8,256]{2,1,0:T(8,128)S(1)}, f32[2,8,256]{2,1,0:T(8,128)S(1)}, f32[2,8,256,128]{3,2,1,0:T(8,128)})) conditional(s32[]{:T(128)} %convert_element_type.148, (f32[2,8,256]{2,1,0:T(8,128)S(1)}, f32[2,8,256]{2,1,0:T(8,128)S(1)}, f32[2,8,256,128]{3,2,1,0:T(8,128)}) %tuple.99, (pred[512]{0:T(512)(128)(4,1)S(1)}, s32[512]{0:T(512)S(1)}, ...), branch_computations={%region_2.2_spmd, %region_3.5_spmd} | conditional | flops 1102323968 | bytes 49550944 | solution.py:103
  274.4 3.5 %multiply_add_fusion = f32[2,8,256,128]{3,2,1,0:T(8,128)S(1)} fusion(f32[2,8,256,128]{3,2,1,0:T(8,128)S(1)} %copy-done.1, bf16[512,2,128,1]{0,2,3,1:T(8,128)(2,1)S(1)} %bitcast.130, f32[2,512,256,8]{2,1,3,0:T(8,128)S(1)} %get-tuple-element.479, f32[2,8,256]{2,1,0:T(8,128)S(1)} %max.10, pred[256,512]{0,1:T(8,128)(4,1)S(1)} %compare_and_fusion, ...), kind=kOutput, calls=%fused_computation.11 | convolution fusion | flops 548405248 | bytes 13008896 | tf_op jit(solution)/shard_map/while/body/eval_jaxpr/cond/branch_1_fun/hgqk,khd->hgqd/dot_general | solution.py:95
  280.5 11.0 %conditional.6 = ((f32[2,8,256]{2,1,0:T(8,128)S(1)}, f32[2,8,256]{2,1,0:T(8,128)S(1)}, f32[2,8,256,128]{3,2,1,0:T(8,128)})) conditional(s32[]{:T(128)} %convert_element_type.148, (f32[2,8,256]{2,1,0:T(8,128)S(1)}, f32[2,8,256]{2,1,0:T(8,128)S(1)}, f32[2,8,256,128]{3,2,1,0:T(8,128)}) %tuple.99, (pred[512]{0:T(512)(128)(4,1)S(1)}, s32[512]{0:T(512)S(1)}, ...), branch_computations={%region_2.2_spmd, %region_3.5_spmd} | conditional | flops 1102323968 | bytes 49550944 | solution.py:103
  286.6 3.5 %multiply_add_fusion = f32[2,8,256,128]{3,2,1,0:T(8,128)S(1)} fusion(f32[2,8,256,128]{3,2,1,0:T(8,128)S(1)} %copy-done.1, bf16[512,2,128,1]{0,2,3,1:T(8,128)(2,1)S(1)} %bitcast.130, f32[2,512,256,8]{2,1,3,0:T(8,128)S(1)} %get-tuple-element.479, f32[2,8,256]{2,1,0:T(8,128)S(1)} %max.10, pred[256,512]{0,1:T(8,128)(4,1)S(1)} %compare_and_fusion, ...), kind=kOutput, calls=%fused_computation.11 | convolution fusion | flops 548405248 | bytes 13008896 | tf_op jit(solution)/shard_map/while/body/eval_jaxpr/cond/branch_1_fun/hgqk,khd->hgqd/dot_general | solution.py:95
  292.8 11.0 %conditional.6 = ((f32[2,8,256]{2,1,0:T(8,128)S(1)}, f32[2,8,256]{2,1,0:T(8,128)S(1)}, f32[2,8,256,128]{3,2,1,0:T(8,128)})) conditional(s32[]{:T(128)} %convert_element_type.148, (f32[2,8,256]{2,1,0:T(8,128)S(1)}, f32[2,8,256]{2,1,0:T(8,128)S(1)}, f32[2,8,256,128]{3,2,1,0:T(8,128)}) %tuple.99, (pred[512]{0:T(512)(128)(4,1)S(1)}, s32[512]{0:T(512)S(1)}, ...), branch_computations={%region_2.2_spmd, %region_3.5_spmd} | conditional | flops 1102323968 | bytes 49550944 | solution.py:103
  298.9 3.5 %multiply_add_fusion = f32[2,8,256,128]{3,2,1,0:T(8,128)S(1)} fusion(f32[2,8,256,128]{3,2,1,0:T(8,128)S(1)} %copy-done.1, bf16[512,2,128,1]{0,2,3,1:T(8,128)(2,1)S(1)} %bitcast.130, f32[2,512,256,8]{2,1,3,0:T(8,128)S(1)} %get-tuple-element.479, f32[2,8,256]{2,1,0:T(8,128)S(1)} %max.10, pred[256,512]{0,1:T(8,128)(4,1)S(1)} %compare_and_fusion, ...), kind=kOutput, calls=%fused_computation.11 | convolution fusion | flops 548405248 | bytes 13008896 | tf_op jit(solution)/shard_map/while/body/eval_jaxpr/cond/branch_1_fun/hgqk,khd->hgqd/dot_general | solution.py:95
  312.1 3.6 %gather_fusion = bf16[128,2048]{1,0:T(8,128)(2,1)} fusion(bf16[256,2048]{1,0:T(8,128)(2,1)} %bitcast.42, s32[1024]{0:T(1024)S(1)} %pad_clamp_fusion), kind=kCustom, calls=%fused_computation.2 | custom fusion | bytes 1049088 | tf_op jit(solution)/shard_map/gather | solution.py:241
  (181 shorter events, 96.9 us)
Async XLA Ops:
  7.2 235.6 %copy-start = (bf16[1,768,2048]{2,1,0:T(8,128)(2,1)S(1)}, bf16[1,768,2048]{2,1,0:T(8,128)(2,1)}, u32[]{:S(2)}) copy-start(bf16[1,768,2048]{2,1,0:T(8,128)(2,1)} %param.35) | copy-start | bytes 9437188
  7.2 38.4 %copy-start.5 = (bf16[1,1,128,256]{3,2,1,0:T(8,128)(2,1)S(1)}, bf16[1,1,128,256]{3,2,1,0:T(8,128)(2,1)}, u32[]{:S(2)}) copy-start(bf16[1,1,128,256]{3,2,1,0:T(8,128)(2,1)} %param.28) | copy-start | bytes 196612
  7.2 38.8 %copy-start.10 = (bf16[1,1,128,256]{3,2,1,0:T(8,128)(2,1)S(1)}, bf16[1,1,128,256]{3,2,1,0:T(8,128)(2,1)}, u32[]{:S(2)}) copy-start(bf16[1,1,128,256]{3,2,1,0:T(8,128)(2,1)} %param.30) | copy-start | bytes 196612
  7.2 40.4 %copy-start.12 = (s32[2,1]{0,1:T(1,128)S(1)}, s32[2,1]{0,1:T(1,128)}, u32[]{:S(2)}) copy-start(s32[2,1]{0,1:T(1,128)} %param.27) | copy-start | bytes 28
  9.0 4.6 %collective-permute-start.1 = (bf16[1,1,256,256]{2,3,1,0:T(8,128)(2,1)}, bf16[1,1,256,256]{2,3,1,0:T(8,128)(2,1)S(1)}, u32[]{:S(2)}, u32[]{:S(2)}) collective-permute-start(bf16[1,1,256,256]{2,3,1,0:T(8,128)(2,1)} %copy.74), channel_id=1, source_target_pairs={{0,16},{16,0},{1,17},{17,1},{2,18},{18,2},{3,19},{19,3},{4,20},{20... | collective-permute-start | bytes 393224 | tf_op jit(solution)/shard_map/ppermute | solution.py:21
  11.9 4.0 %collective-permute-start = (bf16[1,1,256,256]{2,3,1,0:T(8,128)(2,1)}, bf16[1,1,256,256]{2,3,1,0:T(8,128)(2,1)S(1)}, u32[]{:S(2)}, u32[]{:S(2)}) collective-permute-start(bf16[1,1,256,256]{2,3,1,0:T(8,128)(2,1)} %copy.71), channel_id=1, source_target_pairs={{0,16},{16,0},{1,17},{17,1},{2,18},{18,2},{3,19},{19,3},{4,20},{20... | collective-permute-start | bytes 393224 | tf_op jit(solution)/shard_map/ppermute | solution.py:21
  39.3 17.9 %all-to-all-start.1 = ((bf16[256,8,128]{2,0,1:T(8,128)(2,1)}), bf16[256,8,128]{2,0,1:T(8,128)(2,1)}, u32[]{:S(2)}, u32[]{:S(2)}) async-start(bf16[256,8,128]{2,0,1:T(8,128)(2,1)} %get-tuple-element.485), calls=%async_computation.1 | async-start | bytes 1048576 | tf_op jit(solution)/shard_map/all_to_all | solution.py:156
  45.6 97.2 %reduce-scatter.2.cloned.1.call-start = ((), (), s32[]{:S(2)}) async-start(), calls=%async_computation.7 | async-start | bytes 589824 | tf_op jit(solution)/shard_map/reduce_scatter | solution.py:202
  57.2 22.1 %copy-start.8 = (s32[1,1,16,8]{2,3,1,0:T(8,128)S(1)}, s32[1,1,16,8]{2,3,1,0:T(8,128)}, u32[]{:S(2)}) copy-start(s32[1,1,16,8]{2,3,1,0:T(8,128)} %param.36) | copy-start | bytes 1540
  57.3 85.5 %copy-start.3 = (bf16[1,1,16,2048]{3,2,1,0:T(8,128)(2,1)S(1)}, bf16[1,1,16,2048]{3,2,1,0:T(8,128)(2,1)}, u32[]{:S(2)}) copy-start(bf16[1,1,16,2048]{3,2,1,0:T(8,128)(2,1)} %param.31) | copy-start | bytes 196612
  74.5 85.0 %copy-start.11 = (f32[1,1,16,8]{2,3,1,0:T(8,128)S(1)}, f32[1,1,16,8]{2,3,1,0:T(8,128)}, u32[]{:S(2)}) copy-start(f32[1,1,16,8]{2,3,1,0:T(8,128)} %param.37) | copy-start | bytes 1540
  78.6 115.8 %all-gather.3.cloned.1.call-start = ((), (), s32[]{:S(2)}) async-start(), calls=%async_computation.5 | async-start | bytes 1179648 | tf_op jit(solution)/shard_map/all_gather | solution.py:158
  146.1 91.7 %all-to-all-start.2 = ((bf16[16,16,2048]{2,1,0:T(8,128)(2,1)}), bf16[16,16,2048]{2,1,0:T(8,128)(2,1)}, u32[]{:S(2)}, u32[]{:S(2)}) async-start(bf16[16,16,2048]{2,1,0:T(8,128)(2,1)} %bitcast.131), calls=%async_computation.3 | async-start | bytes 2097152 | tf_op jit(solution)/shard_map/all_to_all | solution.py:233
  154.0 81.5 %all-gather.5.cloned.1.call-start = ((), (), s32[]{:S(2)}) async-start(), calls=%async_computation.6 | async-start | bytes 1179648 | tf_op jit(solution)/shard_map/all_gather | solution.py:159
  244.8 67.3 %all-to-all-start.3 = ((bf16[16,16,2048]{2,1,0:T(8,128)(2,1)}), bf16[16,16,2048]{2,1,0:T(8,128)(2,1)}, u32[]{:S(2)}, u32[]{:S(2)}) async-start(bf16[16,16,2048]{2,1,0:T(8,128)(2,1)} %bitcast.134), calls=%async_computation.4 | async-start | bytes 2097152 | tf_op jit(solution)/shard_map/all_to_all | solution.py:240
  260.0 2.1 copy-start.1
  265.6 1.3 copy-start.2
  272.3 2.1 copy-start.1
  277.8 1.3 copy-start.2
  284.6 2.1 copy-start.1
  290.1 1.3 copy-start.2
  296.8 2.1 copy-start.1
  302.4 1.3 copy-start.2
  305.7 11.5 %copy-start.4 = (bf16[16,2048]{1,0:T(8,128)(2,1)S(1)}, bf16[16,2048]{1,0:T(8,128)(2,1)}, u32[]{:S(2)}) copy-start(bf16[16,2048]{1,0:T(8,128)(2,1)} %reduce-scatter.2.cloned.1.call-done) | copy-start | bytes 196612
  (3 other events, 1.9 us)
Sparse Core Ops, SparseCore 0:
  78.7 64.0 reduce-scatter.1
  144.9 49.4 all-gather.2
  196.5 38.9 all-gather.4
where the time goes:
time: 326 us; the launch traced here: 324 us
  waiting for transfers between devices  146 us (45%)
  matrix products  44 us (13%)
  local copies, waits for them, and re-layouts  40.7 us (12%)
  other arithmetic  32.3 us (10%)
  starting transfers between devices  24 us (7%)
  blocking collectives  16.7 us (5%)
  between operations  14.6 us (4%)
  loops' own time  5.96 us (2%)
    reduce_scatter x1, waiting for transfers between devices, body(): lax.psum_scatter(jnp.dot(dec_attn, w_out, preferred_element_type=jnp.floa...  61.8 us
    all_gather x1, waiting for transfers between devices, body(): value_piece = lax.all_gather(prompt_values, 'ctx', axis=2, tiled=True)  38.9 us
    all_gather x1, waiting for transfers between devices, body(): key_piece = lax.all_gather(prompt_keys, 'ctx', axis=2, tiled=True)  33.7 us
    all_to_all x1, blocking collectives, body(): lax.all_to_all(key_chosen, 'ctx', split_axis=1, concat_axis=0, tiled=True)  16.7 us
    unnamed x32, local copies, waits for them, and re-layouts  14.8 us
    dot_general x4, matrix products, prefill_compute(): jnp.einsum('hgqk,khd->hgqd', weights.astype(jnp.bfloat16), value_parts, p...  13.8 us
    dot_general x4, matrix products, prefill_compute(): jnp.einsum('qhgd,khd->hgqk', query_tensor, key_parts, preferred_element_t...  10.9 us
    all_to_all x1, waiting for transfers between devices, body(): lax.all_to_all(value_chosen, 'ctx', split_axis=1, concat_axis=0, tiled=True)  8.31 us
  transfers between devices with their start and end apart: 8, of which 6 were waited for; matrix products, arithmetic and copies ran while one was open for 22% of the time, Pallas kernels for 0%

commit v1 on v0

--- a/solution.py
+++ b/solution.py
@@ -156,7 +156,12 @@
         lax.all_to_all(value_chosen, "ctx", split_axis=1, concat_axis=0, tiled=True),
     )
     key_piece = lax.all_gather(prompt_keys, "ctx", axis=2, tiled=True)
-    value_piece = lax.all_gather(prompt_values, "ctx", axis=2, tiled=True)
+    ring = [prompt_values]
+    for hop in range(7):
+        ring.append(lax.ppermute(ring[-1], "ctx", [(dev, (dev + 1) % 8) for dev in range(8)]))
+    value_piece = jnp.roll(
+        jnp.concatenate(ring[::-1], axis=2), (lax.axis_index("ctx") + 1) * ring[0].shape[2], axis=2
+    )
     row_count = key_piece.shape[2]
     positions = lax.iota(jnp.int32, row_count)
     pre_state = blockwise(

time: 326 us -> 289 us (0.89)
  waiting for transfers between devices: 146 us -> 56.1 us
  local copies, waits for them, and re-layouts: 40.7 us -> 66 us
  starting transfers between devices: 24 us -> 43.2 us
  other arithmetic: 32.3 us -> 40.4 us
    reduce_scatter x1, waiting for transfers between devices: 61.8 us -> 16.2 us  [body(): lax.psum_scatter(jnp.dot(dec_attn, w_out, preferred_element_type=jnp.floa...]
    all_gather x1 -> x0, waiting for transfers between devices: 38.9 us -> none  [body(): value_piece = lax.all_gather(prompt_values, 'ctx', axis=2, tiled=True)]
    ppermute x0 -> x7, starting transfers between devices: none -> 19.2 us  [body(): lax.ppermute(ring[-1], 'ctx', [(dev, (dev + 1) % 8) for dev in range(8)])]
    unnamed x32 -> x55, local copies, waits for them, and re-layouts: 14.8 us -> 32.8 us
    all_gather x1, waiting for transfers between devices: 33.7 us -> 17 us  [body(): key_piece = lax.all_gather(prompt_keys, 'ctx', axis=2, tiled=True)]
    ppermute x0 -> x7, waiting for transfers between devices: none -> 10.2 us  [body(): lax.ppermute(ring[-1], 'ctx', [(dev, (dev + 1) % 8) for dev in range(8)])]
    add x3, other arithmetic: 0.05 us -> 3.77 us  [decode_compute(): run_sum = rescale * run_sum + weights.sum(-1)]
  transfers between devices with their start and end apart: 8 -> 14, of which waited for: 6 -> 10; matrix products, arithmetic and copies ran while one was open for 22% -> 36% of each run, Pallas kernels for 0% -> 0%
where the time goes in v1:
time: 289 us; the launch traced here: 287 us
  local copies, waits for them, and re-layouts  66 us (23%)
  waiting for transfers between devices  56.1 us (19%)
  matrix products  43.9 us (15%)
  starting transfers between devices  43.2 us (15%)
  other arithmetic  40.4 us (14%)
  blocking collectives  16.7 us (6%)
  between operations  15 us (5%)
  loops' own time  5.74 us (2%)
    unnamed x55, local copies, waits for them, and re-layouts  32.8 us
    ppermute x7, starting transfers between devices, body(): lax.ppermute(ring[-1], 'ctx', [(dev, (dev + 1) % 8) for dev in range(8)])  19.2 us
    all_gather x1, waiting for transfers between devices, body(): key_piece = lax.all_gather(prompt_keys, 'ctx', axis=2, tiled=True)  17 us
    all_to_all x1, blocking collectives, body(): lax.all_to_all(key_chosen, 'ctx', split_axis=1, concat_axis=0, tiled=True)  16.7 us
    reduce_scatter x1, waiting for transfers between devices, body(): lax.psum_scatter(jnp.dot(dec_attn, w_out, preferred_element_type=jnp.floa...  16.2 us
    dot_general x4, matrix products, prefill_compute(): jnp.einsum('hgqk,khd->hgqd', weights.astype(jnp.bfloat16), value_parts, p...  13.8 us
    dot_general x4, matrix products, prefill_compute(): jnp.einsum('qhgd,khd->hgqk', query_tensor, key_parts, preferred_element_t...  10.9 us
    ppermute x7, waiting for transfers between devices, body(): lax.ppermute(ring[-1], 'ctx', [(dev, (dev + 1) % 8) for dev in range(8)])  10.2 us
  transfers between devices with their start and end apart: 14, of which 10 were waited for; matrix products, arithmetic and copies ran while one was open for 36% of the time, Pallas kernels for 0%

profile of v1, /device:TPU:25, one launch (start us, length us, event | category | flops | bytes accessed | tf_op | source)
XLA Modules:
  0.0 287.1 jit_solution(11985209274923861438)
XLA Ops:
  20.5 16.7 %all_to_all.40 = bf16[256,8,128]{2,0,1:T(8,128)(2,1)} all-to-all(bf16[256,8,128]{2,0,1:T(8,128)(2,1)S(1)} %get-tuple-element.486), channel_id=1, replica_groups=mesh['group'=2,'ctx'=8,'exp'=2] {'ctx'}, dimensions={1} | all-to-all | bytes 1048576 | tf_op jit(solution)/shard_map/all_to_all | solution.py:155
  37.2 6.3 %all-to-all-start.1 = ((bf16[256,8,128]{2,0,1:T(8,128)(2,1)}), bf16[256,8,128]{2,0,1:T(8,128)(2,1)}, u32[]{:S(2)}, u32[]{:S(2)}) async-start(bf16[256,8,128]{2,0,1:T(8,128)(2,1)} %get-tuple-element.485), calls=%async_computation.1 | async-start | bytes 1048576 | tf_op jit(solution)/shard_map/all_to_all | solution.py:156
  46.0 9.1 %all-to-all-done.1 = bf16[256,8,128]{2,0,1:T(8,128)(2,1)} async-done(((bf16[256,8,128]{2,0,1:T(8,128)(2,1)}), bf16[256,8,128]{2,0,1:T(8,128)(2,1)}, u32[]{:S(2)}, u32[]{:S(2)}) %all-to-all-start.1) | async-done | bytes 524320 | tf_op jit(solution)/shard_map/all_to_all | solution.py:156
  55.7 19.5 %while.31 = (s32[]{:T(128)}, f32[2,128]{1,0:T(2,128)S(1)}, f32[2,128]{1,0:T(2,128)}, f32[2,128,128]{2,1,0:T(8,128)S(1)}, s32[4,512]{1,0:T(4,128)S(1)}, /*index=5...) while((s32[]{:T(128)}, f32[2,128]{1,0:T(2,128)S(1)}, ...), condition=%wide.region_13.15_spmd, body=%wide.region_7.14_spmd.sunk | while | flops 68355584 | bytes 2185460 | solution.py:38
  57.6 4.0 %conditional.5 = ((f32[2,128]{1,0:T(2,128)S(1)}, f32[2,128]{1,0:T(2,128)}, f32[2,128,128]{2,1,0:T(8,128)S(1)})) conditional(s32[]{:T(128)} %convert_element_type.147, (f32[2,128]{1,0:T(2,128)S(1)}, f32[2,128]{1,0:T(2,128)}, f32[2,128,128]{2,1,0:T(8,128)S(1)}) %tuple.95, (pred[1,512]{1,0:T(4,128)(4,1)S(1)}, bf16[4,512,128]{2,1,0:T(8,128)(2,1)}, ...), branch_computations={%region_9.10_spmd, %region_10.13_spmd} | conditional | flops 68354560 | bytes 2182689 | solution.py:131
  63.5 4.0 %conditional.5 = ((f32[2,128]{1,0:T(2,128)S(1)}, f32[2,128]{1,0:T(2,128)}, f32[2,128,128]{2,1,0:T(8,128)S(1)})) conditional(s32[]{:T(128)} %convert_element_type.147, (f32[2,128]{1,0:T(2,128)S(1)}, f32[2,128]{1,0:T(2,128)}, f32[2,128,128]{2,1,0:T(8,128)S(1)}) %tuple.95, (pred[1,512]{1,0:T(4,128)(4,1)S(1)}, bf16[4,512,128]{2,1,0:T(8,128)(2,1)}, ...), branch_computations={%region_9.10_spmd, %region_10.13_spmd} | conditional | flops 68354560 | bytes 2182689 | solution.py:131
  69.3 4.0 %conditional.5 = ((f32[2,128]{1,0:T(2,128)S(1)}, f32[2,128]{1,0:T(2,128)}, f32[2,128,128]{2,1,0:T(8,128)S(1)})) conditional(s32[]{:T(128)} %convert_element_type.147, (f32[2,128]{1,0:T(2,128)S(1)}, f32[2,128]{1,0:T(2,128)}, f32[2,128,128]{2,1,0:T(8,128)S(1)}) %tuple.95, (pred[1,512]{1,0:T(4,128)(4,1)S(1)}, bf16[4,512,128]{2,1,0:T(8,128)(2,1)}, ...), branch_computations={%region_9.10_spmd, %region_10.13_spmd} | conditional | flops 68354560 | bytes 2182689 | solution.py:131
  98.7 4.9 %collective-permute-start.3 = (bf16[1,1,256,256]{3,2,1,0:T(8,128)(2,1)}, bf16[1,1,256,256]{3,2,1,0:T(8,128)(2,1)}, u32[]{:S(2)}, u32[]{:S(2)}) collective-permute-start(bf16[1,1,256,256]{3,2,1,0:T(8,128)(2,1)} %collective-permute-done.2), channel_id=1, source_target_pairs={{0,2},{2,4},{4,6},{6,8},{8,10},{10,12},{12,14},{14,0},{1,3},{3,5},... | collective-permute-start | bytes 393224 | tf_op jit(solution)/shard_map/ppermute | solution.py:161
  117.5 3.8 %collective-permute-start.6 = (bf16[1,1,256,256]{3,2,1,0:T(8,128)(2,1)}, bf16[1,1,256,256]{3,2,1,0:T(8,128)(2,1)}, u32[]{:S(2)}, u32[]{:S(2)}) collective-permute-start(bf16[1,1,256,256]{3,2,1,0:T(8,128)(2,1)} %collective-permute-done.5), channel_id=1, source_target_pairs={{0,2},{2,4},{4,6},{6,8},{8,10},{10,12},{12,14},{14,0},{1,3},{3,5},... | collective-permute-start | bytes 393224 | tf_op jit(solution)/shard_map/ppermute | solution.py:161
  130.2 16.2 %reduce-scatter.2.cloned.1.call-done = bf16[16,2048]{1,0:T(8,128)(2,1)} async-done(((bf16[128,2048]{1,0:T(8,128)(2,1)}), bf16[16,2048]{1,0:T(8,128)(2,1)}) %reduce-scatter.2.cloned.1.call-update) | async-done | bytes 65552 | tf_op jit(solution)/shard_map/reduce_scatter | solution.py:207
  149.8 7.9 %all-to-all-start.2 = ((bf16[16,16,2048]{2,1,0:T(8,128)(2,1)}), bf16[16,16,2048]{2,1,0:T(8,128)(2,1)}, u32[]{:S(2)}, u32[]{:S(2)}) async-start(bf16[16,16,2048]{2,1,0:T(8,128)(2,1)} %bitcast.132), calls=%async_computation.3 | async-start | bytes 2097152 | tf_op jit(solution)/shard_map/all_to_all | solution.py:238
  181.2 17.0 %all-gather.2.cloned.1.call-done = bf16[1,1,2048,256]{3,2,1,0:T(8,128)(2,1)} async-done(((bf16[1,1,256,256]{3,2,1,0:T(8,128)(2,1)}), bf16[1,1,2048,256]{3,2,1,0:T(8,128)(2,1)}) %all-gather.2.cloned.1.call-update) | async-done | bytes 1048592 | tf_op jit(solution)/shard_map/all_gather | solution.py:158
  200.4 4.9 %fusion.28 = f32[256,1536]{1,0:T(8,128)S(1)} fusion(bf16[256,2048]{1,0:T(8,128)(2,1)} %bitcast.38, bf16[1,2048,1536]{2,1,0:T(8,128)(2,1)} %param.34), kind=kOutput, calls=%fused_computation.43 | convolution fusion | flops 1610612736 | bytes 8912896 | tf_op jit(solution)/shard_map/dot_general | solution.py:240
  207.4 8.3 %all-to-all-start.3 = ((bf16[16,16,2048]{2,1,0:T(8,128)(2,1)}), bf16[16,16,2048]{2,1,0:T(8,128)(2,1)}, u32[]{:S(2)}, u32[]{:S(2)}) async-start(bf16[16,16,2048]{2,1,0:T(8,128)(2,1)} %bitcast.136), calls=%async_computation.4 | async-start | bytes 2097152 | tf_op jit(solution)/shard_map/all_to_all | solution.py:245
  217.2 48.9 %while.32 = (s32[]{:T(128)}, f32[2,8,256]{2,1,0:T(8,128)S(1)}, f32[2,8,256]{2,1,0:T(8,128)S(1)}, f32[2,8,256,128]{3,2,1,0:T(8,128)}, s32[4,512]{1,0:T(4,128)S(1)...) while((s32[]{:T(128)}, f32[2,8,256]{2,1,0:T(8,128)S(1)}, ...), condition=%wide.region_6.7_spmd.clone, body=%wide.region_0.0_spmd.clone.sunk | while | flops 1102324992 | bytes 49558864 | solution.py:38
  218.5 10.9 %conditional.6 = ((f32[2,8,256]{2,1,0:T(8,128)S(1)}, f32[2,8,256]{2,1,0:T(8,128)S(1)}, f32[2,8,256,128]{3,2,1,0:T(8,128)})) conditional(s32[]{:T(128)} %convert_element_type.148, (f32[2,8,256]{2,1,0:T(8,128)S(1)}, f32[2,8,256]{2,1,0:T(8,128)S(1)}, f32[2,8,256,128]{3,2,1,0:T(8,128)}) %tuple.99, (pred[512]{0:T(512)(128)(4,1)S(1)}, s32[512]{0:T(512)S(1)}, ...), branch_computations={%region_2.2_spmd, %region_3.5_spmd} | conditional | flops 1102323968 | bytes 49550944 | solution.py:103
  224.6 3.5 %multiply_add_fusion = f32[2,8,256,128]{3,2,1,0:T(8,128)S(1)} fusion(f32[2,8,256,128]{3,2,1,0:T(8,128)S(1)} %copy-done.1, bf16[512,2,128,1]{0,2,3,1:T(8,128)(2,1)S(1)} %bitcast.130, f32[2,512,256,8]{2,1,3,0:T(8,128)S(1)} %get-tuple-element.479, f32[2,8,256]{2,1,0:T(8,128)S(1)} %max.10, pred[256,512]{0,1:T(8,128)(4,1)S(1)} %compare_and_fusion, ...), kind=kOutput, calls=%fused_computation.11 | convolution fusion | flops 548405248 | bytes 13008896 | tf_op jit(solution)/shard_map/while/body/eval_jaxpr/cond/branch_1_fun/hgqk,khd->hgqd/dot_general | solution.py:95
  230.7 10.9 %conditional.6 = ((f32[2,8,256]{2,1,0:T(8,128)S(1)}, f32[2,8,256]{2,1,0:T(8,128)S(1)}, f32[2,8,256,128]{3,2,1,0:T(8,128)})) conditional(s32[]{:T(128)} %convert_element_type.148, (f32[2,8,256]{2,1,0:T(8,128)S(1)}, f32[2,8,256]{2,1,0:T(8,128)S(1)}, f32[2,8,256,128]{3,2,1,0:T(8,128)}) %tuple.99, (pred[512]{0:T(512)(128)(4,1)S(1)}, s32[512]{0:T(512)S(1)}, ...), branch_computations={%region_2.2_spmd, %region_3.5_spmd} | conditional | flops 1102323968 | bytes 49550944 | solution.py:103
  236.9 3.5 %multiply_add_fusion = f32[2,8,256,128]{3,2,1,0:T(8,128)S(1)} fusion(f32[2,8,256,128]{3,2,1,0:T(8,128)S(1)} %copy-done.1, bf16[512,2,128,1]{0,2,3,1:T(8,128)(2,1)S(1)} %bitcast.130, f32[2,512,256,8]{2,1,3,0:T(8,128)S(1)} %get-tuple-element.479, f32[2,8,256]{2,1,0:T(8,128)S(1)} %max.10, pred[256,512]{0,1:T(8,128)(4,1)S(1)} %compare_and_fusion, ...), kind=kOutput, calls=%fused_computation.11 | convolution fusion | flops 548405248 | bytes 13008896 | tf_op jit(solution)/shard_map/while/body/eval_jaxpr/cond/branch_1_fun/hgqk,khd->hgqd/dot_general | solution.py:95
  243.0 10.9 %conditional.6 = ((f32[2,8,256]{2,1,0:T(8,128)S(1)}, f32[2,8,256]{2,1,0:T(8,128)S(1)}, f32[2,8,256,128]{3,2,1,0:T(8,128)})) conditional(s32[]{:T(128)} %convert_element_type.148, (f32[2,8,256]{2,1,0:T(8,128)S(1)}, f32[2,8,256]{2,1,0:T(8,128)S(1)}, f32[2,8,256,128]{3,2,1,0:T(8,128)}) %tuple.99, (pred[512]{0:T(512)(128)(4,1)S(1)}, s32[512]{0:T(512)S(1)}, ...), branch_computations={%region_2.2_spmd, %region_3.5_spmd} | conditional | flops 1102323968 | bytes 49550944 | solution.py:103
  249.1 3.5 %multiply_add_fusion = f32[2,8,256,128]{3,2,1,0:T(8,128)S(1)} fusion(f32[2,8,256,128]{3,2,1,0:T(8,128)S(1)} %copy-done.1, bf16[512,2,128,1]{0,2,3,1:T(8,128)(2,1)S(1)} %bitcast.130, f32[2,512,256,8]{2,1,3,0:T(8,128)S(1)} %get-tuple-element.479, f32[2,8,256]{2,1,0:T(8,128)S(1)} %max.10, pred[256,512]{0,1:T(8,128)(4,1)S(1)} %compare_and_fusion, ...), kind=kOutput, calls=%fused_computation.11 | convolution fusion | flops 548405248 | bytes 13008896 | tf_op jit(solution)/shard_map/while/body/eval_jaxpr/cond/branch_1_fun/hgqk,khd->hgqd/dot_general | solution.py:95
  255.2 10.9 %conditional.6 = ((f32[2,8,256]{2,1,0:T(8,128)S(1)}, f32[2,8,256]{2,1,0:T(8,128)S(1)}, f32[2,8,256,128]{3,2,1,0:T(8,128)})) conditional(s32[]{:T(128)} %convert_element_type.148, (f32[2,8,256]{2,1,0:T(8,128)S(1)}, f32[2,8,256]{2,1,0:T(8,128)S(1)}, f32[2,8,256,128]{3,2,1,0:T(8,128)}) %tuple.99, (pred[512]{0:T(512)(128)(4,1)S(1)}, s32[512]{0:T(512)S(1)}, ...), branch_computations={%region_2.2_spmd, %region_3.5_spmd} | conditional | flops 1102323968 | bytes 49550944 | solution.py:103
  261.3 3.5 %multiply_add_fusion = f32[2,8,256,128]{3,2,1,0:T(8,128)S(1)} fusion(f32[2,8,256,128]{3,2,1,0:T(8,128)S(1)} %copy-done.1, bf16[512,2,128,1]{0,2,3,1:T(8,128)(2,1)S(1)} %bitcast.130, f32[2,512,256,8]{2,1,3,0:T(8,128)S(1)} %get-tuple-element.479, f32[2,8,256]{2,1,0:T(8,128)S(1)} %max.10, pred[256,512]{0,1:T(8,128)(4,1)S(1)} %compare_and_fusion, ...), kind=kOutput, calls=%fused_computation.11 | convolution fusion | flops 548405248 | bytes 13008896 | tf_op jit(solution)/shard_map/while/body/eval_jaxpr/cond/branch_1_fun/hgqk,khd->hgqd/dot_general | solution.py:95
  274.5 3.6 %gather_fusion = bf16[128,2048]{1,0:T(8,128)(2,1)} fusion(bf16[256,2048]{1,0:T(8,128)(2,1)} %bitcast.42, s32[1024]{0:T(1024)S(1)} %pad_clamp_fusion), kind=kCustom, calls=%fused_computation.2 | custom fusion | bytes 1049088 | tf_op jit(solution)/shard_map/gather | solution.py:246
  (217 shorter events, 153.8 us)
Async XLA Ops:
  7.2 198.2 %copy-start = (bf16[1,768,2048]{2,1,0:T(8,128)(2,1)S(1)}, bf16[1,768,2048]{2,1,0:T(8,128)(2,1)}, u32[]{:S(2)}) copy-start(bf16[1,768,2048]{2,1,0:T(8,128)(2,1)} %param.35) | copy-start | bytes 9437188
  8.3 4.4 %collective-permute-start.8 = (bf16[1,1,256,256]{2,3,1,0:T(8,128)(2,1)S(1)}, bf16[1,1,256,256]{2,3,1,0:T(8,128)(2,1)S(1)}, u32[]{:S(2)}, u32[]{:S(2)}) collective-permute-start(bf16[1,1,256,256]{2,3,1,0:T(8,128)(2,1)S(1)} %copy.74), channel_id=1, source_target_pairs={{0,16},{16,0},{1,17},{17,1},{2,18},{18,2},{3,19},{19,3},{4,20},{20... | collective-permute-start | bytes 393224 | tf_op jit(solution)/shard_map/ppermute | solution.py:21
  11.3 4.0 %collective-permute-start.7 = (bf16[1,1,256,256]{2,3,1,0:T(8,128)(2,1)}, bf16[1,1,256,256]{2,3,1,0:T(8,128)(2,1)S(1)}, u32[]{:S(2)}, u32[]{:S(2)}) collective-permute-start(bf16[1,1,256,256]{2,3,1,0:T(8,128)(2,1)} %copy.71), channel_id=1, source_target_pairs={{0,16},{16,0},{1,17},{17,1},{2,18},{18,2},{3,19},{19,3},{4,20},{20... | collective-permute-start | bytes 393224 | tf_op jit(solution)/shard_map/ppermute | solution.py:21
  18.2 25.3 %copy-start.8 = (bf16[1,1,128,256]{3,2,1,0:T(8,128)(2,1)S(1)}, bf16[1,1,128,256]{3,2,1,0:T(8,128)(2,1)}, u32[]{:S(2)}) copy-start(bf16[1,1,128,256]{3,2,1,0:T(8,128)(2,1)} %param.28) | copy-start | bytes 196612
  18.2 25.7 %copy-start.11 = (bf16[1,1,128,256]{3,2,1,0:T(8,128)(2,1)S(1)}, bf16[1,1,128,256]{3,2,1,0:T(8,128)(2,1)}, u32[]{:S(2)}) copy-start(bf16[1,1,128,256]{3,2,1,0:T(8,128)(2,1)} %param.30) | copy-start | bytes 196612
  18.2 25.7 %copy-start.12 = (bf16[1,1,128,256]{3,2,1,0:T(8,128)(2,1)S(1)}, bf16[1,1,128,256]{3,2,1,0:T(8,128)(2,1)}, u32[]{:S(2)}) copy-start(bf16[1,1,128,256]{3,2,1,0:T(8,128)(2,1)} %param.29) | copy-start | bytes 196612
  18.2 26.5 %copy-start.15 = (s32[2,1]{0,1:T(1,128)S(1)}, s32[2,1]{0,1:T(1,128)}, u32[]{:S(2)}) copy-start(s32[2,1]{0,1:T(1,128)} %param.27) | copy-start | bytes 28
  37.2 17.9 %all-to-all-start.1 = ((bf16[256,8,128]{2,0,1:T(8,128)(2,1)}), bf16[256,8,128]{2,0,1:T(8,128)(2,1)}, u32[]{:S(2)}, u32[]{:S(2)}) async-start(bf16[256,8,128]{2,0,1:T(8,128)(2,1)} %get-tuple-element.485), calls=%async_computation.1 | async-start | bytes 1048576 | tf_op jit(solution)/shard_map/all_to_all | solution.py:156
  43.5 103.0 %reduce-scatter.2.cloned.1.call-start = ((), (), s32[]{:S(2)}) async-start(), calls=%async_computation.6 | async-start | bytes 589824 | tf_op jit(solution)/shard_map/reduce_scatter | solution.py:207
  75.2 9.7 %copy-start.9 = (s32[1,1,16,8]{2,3,1,0:T(8,128)S(1)}, s32[1,1,16,8]{2,3,1,0:T(8,128)}, u32[]{:S(2)}) copy-start(s32[1,1,16,8]{2,3,1,0:T(8,128)} %param.36) | copy-start | bytes 1540
  79.3 118.8 %all-gather.2.cloned.1.call-start = ((), (), s32[]{:S(2)}) async-start(), calls=%async_computation.5 | async-start | bytes 1179648 | tf_op jit(solution)/shard_map/all_gather | solution.py:158
  79.4 4.8 %collective-permute-start = (bf16[1,1,256,256]{3,2,1,0:T(8,128)(2,1)S(1)}, bf16[1,1,256,256]{3,2,1,0:T(8,128)(2,1)S(1)}, u32[]{:S(2)}, u32[]{:S(2)}) collective-permute-start(bf16[1,1,256,256]{3,2,1,0:T(8,128)(2,1)S(1)} %copy-done.3), channel_id=1, source_target_pairs={{0,2},{2,4},{4,6},{6,8},{8,10},{10,12},{12,14},{14,0},{1,3},{3,5},... | collective-permute-start | bytes 393224 | tf_op jit(solution)/shard_map/ppermute | solution.py:161
  84.1 5.1 %collective-permute-start.1 = (bf16[1,1,256,256]{3,2,1,0:T(8,128)(2,1)S(1)}, bf16[1,1,256,256]{3,2,1,0:T(8,128)(2,1)S(1)}, u32[]{:S(2)}, u32[]{:S(2)}) collective-permute-start(bf16[1,1,256,256]{3,2,1,0:T(8,128)(2,1)S(1)} %collective-permute-done), channel_id=1, source_target_pairs={{0,2},{2,4},{4,6},{6,8},{8,10},{10,12},{12,14},{14,0},{1,3},{3,5},... | collective-permute-start | bytes 393224 | tf_op jit(solution)/shard_map/ppermute | solution.py:161
  89.3 33.2 %copy-start.6 = (bf16[1,1,256,256]{3,2,1,0:T(8,128)(2,1)}, bf16[1,1,256,256]{3,2,1,0:T(8,128)(2,1)S(1)}, u32[]{:S(2)}) copy-start(bf16[1,1,256,256]{3,2,1,0:T(8,128)(2,1)S(1)} %collective-permute-done.1) | copy-start | bytes 393220
  89.3 9.4 %collective-permute-start.2 = (bf16[1,1,256,256]{3,2,1,0:T(8,128)(2,1)S(1)}, bf16[1,1,256,256]{3,2,1,0:T(8,128)(2,1)}, u32[]{:S(2)}, u32[]{:S(2)}) collective-permute-start(bf16[1,1,256,256]{3,2,1,0:T(8,128)(2,1)S(1)} %collective-permute-done.1), channel_id=1, source_target_pairs={{0,2},{2,4},{4,6},{6,8},{8,10},{10,12},{12,14},{14,0},{1,3},{3,5},... | collective-permute-start | bytes 393224 | tf_op jit(solution)/shard_map/ppermute | solution.py:161
  98.7 7.3 %collective-permute-start.3 = (bf16[1,1,256,256]{3,2,1,0:T(8,128)(2,1)}, bf16[1,1,256,256]{3,2,1,0:T(8,128)(2,1)}, u32[]{:S(2)}, u32[]{:S(2)}) collective-permute-start(bf16[1,1,256,256]{3,2,1,0:T(8,128)(2,1)} %collective-permute-done.2), channel_id=1, source_target_pairs={{0,2},{2,4},{4,6},{6,8},{8,10},{10,12},{12,14},{14,0},{1,3},{3,5},... | collective-permute-start | bytes 393224 | tf_op jit(solution)/shard_map/ppermute | solution.py:161
  106.0 5.4 %collective-permute-start.4 = (bf16[1,1,256,256]{3,2,1,0:T(8,128)(2,1)}, bf16[1,1,256,256]{3,2,1,0:T(8,128)(2,1)}, u32[]{:S(2)}, u32[]{:S(2)}) collective-permute-start(bf16[1,1,256,256]{3,2,1,0:T(8,128)(2,1)} %collective-permute-done.3), channel_id=1, source_target_pairs={{0,2},{2,4},{4,6},{6,8},{8,10},{10,12},{12,14},{14,0},{1,3},{3,5},... | collective-permute-start | bytes 393224 | tf_op jit(solution)/shard_map/ppermute | solution.py:161
  111.4 6.1 %collective-permute-start.5 = (bf16[1,1,256,256]{3,2,1,0:T(8,128)(2,1)}, bf16[1,1,256,256]{3,2,1,0:T(8,128)(2,1)}, u32[]{:S(2)}, u32[]{:S(2)}) collective-permute-start(bf16[1,1,256,256]{3,2,1,0:T(8,128)(2,1)} %collective-permute-done.4), channel_id=1, source_target_pairs={{0,2},{2,4},{4,6},{6,8},{8,10},{10,12},{12,14},{14,0},{1,3},{3,5},... | collective-permute-start | bytes 393224 | tf_op jit(solution)/shard_map/ppermute | solution.py:161
  117.5 11.2 %collective-permute-start.6 = (bf16[1,1,256,256]{3,2,1,0:T(8,128)(2,1)}, bf16[1,1,256,256]{3,2,1,0:T(8,128)(2,1)}, u32[]{:S(2)}, u32[]{:S(2)}) collective-permute-start(bf16[1,1,256,256]{3,2,1,0:T(8,128)(2,1)} %collective-permute-done.5), channel_id=1, source_target_pairs={{0,2},{2,4},{4,6},{6,8},{8,10},{10,12},{12,14},{14,0},{1,3},{3,5},... | collective-permute-start | bytes 393224 | tf_op jit(solution)/shard_map/ppermute | solution.py:161
  123.2 23.3 %copy-start.4 = (bf16[1,1,16,2048]{3,2,1,0:T(8,128)(2,1)S(1)}, bf16[1,1,16,2048]{3,2,1,0:T(8,128)(2,1)}, u32[]{:S(2)}) copy-start(bf16[1,1,16,2048]{3,2,1,0:T(8,128)(2,1)} %param.31) | copy-start | bytes 196612
  149.8 50.6 %all-to-all-start.2 = ((bf16[16,16,2048]{2,1,0:T(8,128)(2,1)}), bf16[16,16,2048]{2,1,0:T(8,128)(2,1)}, u32[]{:S(2)}, u32[]{:S(2)}) async-start(bf16[16,16,2048]{2,1,0:T(8,128)(2,1)} %bitcast.132), calls=%async_computation.3 | async-start | bytes 2097152 | tf_op jit(solution)/shard_map/all_to_all | solution.py:238
  157.7 17.0 %copy-start.7 = (bf16[1,1,256,256]{3,2,1,0:T(8,128)(2,1)S(1)}, bf16[1,1,256,256]{3,2,1,0:T(8,128)(2,1)}, u32[]{:S(2)}) copy-start(bf16[1,1,256,256]{3,2,1,0:T(8,128)(2,1)} %copy-done.6) | copy-start | bytes 393220
  207.4 67.1 %all-to-all-start.3 = ((bf16[16,16,2048]{2,1,0:T(8,128)(2,1)}), bf16[16,16,2048]{2,1,0:T(8,128)(2,1)}, u32[]{:S(2)}, u32[]{:S(2)}) async-start(bf16[16,16,2048]{2,1,0:T(8,128)(2,1)} %bitcast.136), calls=%async_computation.4 | async-start | bytes 2097152 | tf_op jit(solution)/shard_map/all_to_all | solution.py:245
  274.5 5.1 %copy-start.5 = (bf16[16,2048]{1,0:T(8,128)(2,1)S(1)}, bf16[16,2048]{1,0:T(8,128)(2,1)}, u32[]{:S(2)}) copy-start(bf16[16,2048]{1,0:T(8,128)(2,1)} %reduce-scatter.2.cloned.1.call-done) | copy-start | bytes 196612
  (13 other events, 34.7 us)
Sparse Core Ops, SparseCore 0:
  79.4 67.0 reduce-scatter.1
  148.6 49.4 all-gather.1
